TPU v7x, 32 devices: a whole 2x2x4 slice. The times are simulated.
32 devices in a mesh: row: 8 (over y, x, core), col: 4 (over z).
Axes of the slice: x: 2, y: 2, z: 4, core: 2. Of those that a mesh axis runs over, the one named last changes fastest.
Arguments:
- left_factors: float32 [128, 256, 32], P(None, ('row', 'col')), may hold values from -12 to 12
- right_factors: float32 [128, 128, 32], P(None, ('col', 'row')), may hold values from -12 to 12
- weight: float32 [1024, 128], replicated, may hold values from -0.1875 to 0.1875
- bias: float32 [128], replicated, may hold values from -2 to 2
- cotangent: float32 [256, 128, 128], P('row', 'col'), may hold values from -6 to 6
Outputs:
- pair_out: float32 [256, 128, 128], P('row', 'col')
- left_grad: float32 [128, 256, 32], P(None, ('row', 'col'))
- right_grad: float32 [128, 128, 32], P(None, ('col', 'row'))
- weight_grad: float32 [1024, 128], replicated
- bias_grad: float32 [128], replicated
All inputs are finite; a program needn't handle non-finite values.
Results may differ from a plain program's by a relative error of at most 0.0001.
Values sent between devices are 32-bit elements; how exact they have to be, the bound alone decides.
A program may use at most 64 MiB of HBM per device.

v0:
```python
import jax
import jax.numpy as jnp
from jax import lax
from jax.sharding import PartitionSpec as P


def per_device(left_factors, right_factors, weight, bias, cotangent):
    high = lax.Precision.HIGHEST
    samples = left_factors.shape[0]
    width = left_factors.shape[2]
    pair_width = weight.shape[1]
    left_all = lax.all_gather(left_factors, "col", axis=1, tiled=True)
    right_all = lax.all_gather(right_factors, "row", axis=1, tiled=True)
    tile_rows = left_all.shape[1]
    tile_cols = right_all.shape[1]
    step_rows = 16
    blocks = tile_rows // step_rows
    left_blocks = left_all.reshape(samples, blocks, step_rows, width).transpose(1, 0, 2, 3)
    cot_blocks = cotangent.reshape(blocks, step_rows, tile_cols, pair_width)

    def visit(carry, item):
        weight_sum, right_sum = carry
        left_block, cot_block = item
        outer = jnp.einsum("sic,sjd->ijcd", left_block, right_all, precision=high) / samples
        flat = outer.reshape(step_rows, tile_cols, width * width)
        pair_block = jnp.einsum("ijk,ke->ije", flat, weight, precision=high) + bias
        grad_flat = jnp.einsum("ije,ke->ijk", cot_block, weight, precision=high)
        weight_sum = weight_sum + jnp.einsum("ijk,ije->ke", flat, cot_block, precision=high)
        grad_outer = grad_flat.reshape(step_rows, tile_cols, width, width)
        left_block_grad = (
            jnp.einsum("ijcd,sjd->sic", grad_outer, right_all, precision=high) / samples
        )
        right_sum = (
            right_sum
            + jnp.einsum("ijcd,sic->sjd", grad_outer, left_block, precision=high) / samples
        )
        return ((weight_sum, right_sum), (pair_block, left_block_grad))

    start = (
        jnp.zeros((width * width, pair_width), jnp.float32),
        jnp.zeros((samples, tile_cols, width), jnp.float32),
    )
    (weight_part, right_part), (pair_blocks, left_pieces) = lax.scan(
        visit, start, (left_blocks, cot_blocks)
    )
    pair_out = pair_blocks.reshape(tile_rows, tile_cols, pair_width)
    left_part = left_pieces.transpose(1, 0, 2, 3).reshape(samples, tile_rows, width)
    bias_part = jnp.sum(cotangent, axis=(0, 1))
    left_total = lax.psum(left_part, "col")
    right_total = lax.psum(right_part, "row")
    left_share = tile_rows // lax.axis_size("col")
    right_share = tile_cols // lax.axis_size("row")
    left_grad = lax.dynamic_slice_in_dim(
        left_total, lax.axis_index("col") * left_share, left_share, 1
    )
    right_grad = lax.dynamic_slice_in_dim(
        right_total, lax.axis_index("row") * right_share, right_share, 1
    )
    weight_half, bias_half = lax.psum((weight_part, bias_part), "col")
    weight_total, bias_total = lax.psum((weight_half, bias_half), "row")
    total_rows = tile_rows * lax.axis_size("row")
    weight_grad = weight_total / total_rows
    bias_grad = bias_total / total_rows
    return (pair_out, left_grad, right_grad, weight_grad, bias_grad)


def solution(mesh):
    in_specs = (
        P(None, ("row", "col"), None),
        P(None, ("col", "row"), None),
        P(),
        P(),
        P("row", "col", None),
    )
    out_specs = (
        P("row", "col", None),
        P(None, ("row", "col"), None),
        P(None, ("col", "row"), None),
        P(),
        P(),
    )
    return jax.shard_map(
        per_device, mesh=mesh, in_specs=in_specs, out_specs=out_specs, check_vma=False
    )
```

profile of v0, /device:TPU:0, one launch (start us, length us, event | category | flops | bytes accessed | tf_op | source)
XLA Modules:
  0.0 329.0 jit_solution(1549016555022079670)
XLA Ops:
  7.2 0.0 all-reduce.7.cloned.1.call-start
  7.2 11.6 %all_gather.7 = f32[128,32,32]{0,2,1:T(8,128)S(1)} all-gather(f32[128,4,32]{0,2,1:T(8,128)} %param.8), channel_id=1, replica_groups=mesh['row'=8,'col'=4] {'row'}, dimensions={1}, use_global_device_ids=true | all-gather | bytes 589824 | tf_op jit(solution)/shard_map/all_gather | solution.py:13
  18.9 0.3 copy.17
  19.2 16.6 %all_gather.6 = f32[128,32,32]{0,2,1:T(8,128)S(1)} all-gather(f32[128,8,32]{0,2,1:T(8,128)} %param.7), channel_id=1, replica_groups=mesh['row'=8,'col'=4] {'col'}, dimensions={1}, use_global_device_ids=true | all-gather | bytes 655360 | tf_op jit(solution)/shard_map/all_gather | solution.py:12
  35.7 170.8 %while.17 = (s32[]{:T(128)}, f32[1024,128]{1,0:T(8,128)}, f32[128,32,32]{0,2,1:T(8,128)}, f32[2,16,32,128]{3,2,1,0:T(8,128)}, f32[2,128,16,32]{1,3,2,0:T(8,128)}...) while((s32[]{:T(128)}, f32[1024,128]{1,0:T(8,128)}, ...), condition=%wide.region_1.2_spmd.clone, body=%wide.region_0.1_spmd.clone.sunk | while | flops 4833148928 | bytes 49812356 | solution.py:43
  59.1 0.0 copy-start.2
  59.1 0.8 copy-done.2
  59.9 9.1 %multiply_bitcast_fusion.2 = f32[16,32,32,32]{3,2,1,0:T(8,128)} fusion(f32[128,32,32]{0,1,2:T(8,128)S(1)} %get-tuple-element.222, f32[2,128,16,32]{1,3,2,0:T(8,128)S(1)} %get-tuple-element.221, s32[]{:T(128)} %get-tuple-element.204), kind=kOutput, calls=%fused_computation.2.clone.1 | convolution fusion | flops 805830656 | bytes 2883588 | tf_op jit(solution)/shard_map/while/body/eval_jaxpr/sic,sjd->ijcd/dot_general | solution.py:24
  68.9 6.7 %reshape.43 = f32[16,32,1024]{2,1,0:T(8,128)S(1)} reshape(f32[16,32,32,32]{3,2,1,0:T(8,128)} %multiply_bitcast_fusion.2) | data formatting | bytes 4194304 | tf_op jit(solution)/shard_map/while/body/eval_jaxpr/reshape | solution.py:25
  75.6 0.0 copy-start.4
  75.7 5.2 %fusion.67 = f32[1024,128]{1,0:T(8,128)} fusion(f32[16,32,1024]{2,1,0:T(8,128)S(1)} %reshape.43, f32[1024,128]{1,0:T(8,128)} %get-tuple-element.205, pred[]{:T(512)S(6)} %compare.3, f32[2,16,32,128]{3,2,1,0:T(8,128)} %get-tuple-element.223, s32[]{:T(128)} %get-tuple-element.204), kind=kOutput, calls=%fused_computation.5.clone.1 | convolution fusion | flops 805568512 | bytes 3408385 | tf_op jit(solution)/shard_map/while/body/eval_jaxpr/ijk,ije->ke/dot_general | solution.py:28
  80.9 0.0 copy-done.1
  80.9 7.7 %fusion.68 = f32[16,32,32,32]{3,1,2,0:T(8,128)S(1)} fusion(f32[32,32,128,1]{2,1,0,3:T(8,128)S(1)} %bitcast.110, f32[2,16,32,128]{3,2,1,0:T(8,128)} %get-tuple-element.223, s32[]{:T(128)} %get-tuple-element.204), kind=kOutput, calls=%fused_computation.19.clone.1 | convolution fusion | flops 805306368 | bytes 2884096 | tf_op jit(solution)/shard_map/while/body/eval_jaxpr/ije,ke->ijk/dot_general | solution.py:27
  88.6 0.0 copy-start
  88.6 3.2 copy-done
  91.8 0.0 copy-done.4
  91.8 17.0 %fusion.69 = f32[128,32,32]{0,2,1:T(8,128)S(1)} fusion(f32[16,32,32,32]{3,1,2,0:T(8,128)S(1)} %fusion.68, f32[128,32,32]{0,2,1:T(8,128)S(1)} %copy-done.4, pred[]{:T(512)S(6)} %compare.3, f32[2,128,16,32]{1,3,2,0:T(8,128)} %copy-done.2, s32[]{:T(128)} %get-tuple-element.204), kind=kOutput, calls=%fused_computation.7.clone.1 | convolution fusion | flops 805699584 | bytes 3408385 | tf_op jit(solution)/shard_map/while/body/eval_jaxpr/ijcd,sic->sjd/dot_general | solution.py:35
  108.8 0.0 copy-start.5
  108.8 0.8 copy-done.5
  109.6 2.5 fusion.70
  112.1 10.6 %copy.39 = f32[16,32,32,32]{1,2,3,0:T(8,128)} copy(f32[16,32,32,32]{3,1,2,0:T(8,128)} %copy-done) | data formatting | bytes 4194304 | tf_op jit(solution)/shard_map/while/body/eval_jaxpr/ije,ke->ijk/dot_general | solution.py:27
  122.7 9.2 %fusion.71 = f32[2,128,16,32]{1,3,2,0:T(8,128)S(1)} fusion(f32[2,128,16,32]{1,3,2,0:T(8,128)S(1)} %copy-done.6, s32[]{:T(128)} %get-tuple-element.204, f32[16,32,32,32]{1,2,3,0:T(8,128)} %copy.39, f32[128,32,32]{0,1,2:T(8,128)S(1)} %get-tuple-element.222), kind=kOutput, calls=%fused_computation.14.clone.1 | convolution fusion | flops 805371904 | bytes 2883588 | tf_op jit(solution)/shard_map/while/body/eval_jaxpr/ijcd,sjd->sic/dot_general | solution.py:31
  131.9 0.0 copy-start.7
  131.9 0.8 copy-done.7
  132.7 0.8 copy-done.2
  133.5 9.0 %multiply_bitcast_fusion.2 = f32[16,32,32,32]{3,2,1,0:T(8,128)} fusion(f32[128,32,32]{0,1,2:T(8,128)S(1)} %get-tuple-element.222, f32[2,128,16,32]{1,3,2,0:T(8,128)S(1)} %get-tuple-element.221, s32[]{:T(128)} %get-tuple-element.204), kind=kOutput, calls=%fused_computation.2.clone.1 | convolution fusion | flops 805830656 | bytes 2883588 | tf_op jit(solution)/shard_map/while/body/eval_jaxpr/sic,sjd->ijcd/dot_general | solution.py:24
  142.6 6.7 %reshape.43 = f32[16,32,1024]{2,1,0:T(8,128)S(1)} reshape(f32[16,32,32,32]{3,2,1,0:T(8,128)} %multiply_bitcast_fusion.2) | data formatting | bytes 4194304 | tf_op jit(solution)/shard_map/while/body/eval_jaxpr/reshape | solution.py:25
  149.3 5.4 %fusion.67 = f32[1024,128]{1,0:T(8,128)} fusion(f32[16,32,1024]{2,1,0:T(8,128)S(1)} %reshape.43, f32[1024,128]{1,0:T(8,128)} %get-tuple-element.205, pred[]{:T(512)S(6)} %compare.3, f32[2,16,32,128]{3,2,1,0:T(8,128)} %get-tuple-element.223, s32[]{:T(128)} %get-tuple-element.204), kind=kOutput, calls=%fused_computation.5.clone.1 | convolution fusion | flops 805568512 | bytes 3408385 | tf_op jit(solution)/shard_map/while/body/eval_jaxpr/ijk,ije->ke/dot_general | solution.py:28
  154.7 7.7 %fusion.68 = f32[16,32,32,32]{3,1,2,0:T(8,128)S(1)} fusion(f32[32,32,128,1]{2,1,0,3:T(8,128)S(1)} %bitcast.110, f32[2,16,32,128]{3,2,1,0:T(8,128)} %get-tuple-element.223, s32[]{:T(128)} %get-tuple-element.204), kind=kOutput, calls=%fused_computation.19.clone.1 | convolution fusion | flops 805306368 | bytes 2884096 | tf_op jit(solution)/shard_map/while/body/eval_jaxpr/ije,ke->ijk/dot_general | solution.py:27
  162.4 3.2 copy-done
  165.6 17.0 %fusion.69 = f32[128,32,32]{0,2,1:T(8,128)S(1)} fusion(f32[16,32,32,32]{3,1,2,0:T(8,128)S(1)} %fusion.68, f32[128,32,32]{0,2,1:T(8,128)S(1)} %copy-done.4, pred[]{:T(512)S(6)} %compare.3, f32[2,128,16,32]{1,3,2,0:T(8,128)} %copy-done.2, s32[]{:T(128)} %get-tuple-element.204), kind=kOutput, calls=%fused_computation.7.clone.1 | convolution fusion | flops 805699584 | bytes 3408385 | tf_op jit(solution)/shard_map/while/body/eval_jaxpr/ijcd,sic->sjd/dot_general | solution.py:35
  182.6 0.8 copy-done.5
  183.4 2.5 fusion.70
  185.9 10.6 %copy.39 = f32[16,32,32,32]{1,2,3,0:T(8,128)} copy(f32[16,32,32,32]{3,1,2,0:T(8,128)} %copy-done) | data formatting | bytes 4194304 | tf_op jit(solution)/shard_map/while/body/eval_jaxpr/ije,ke->ijk/dot_general | solution.py:27
  196.5 9.2 %fusion.71 = f32[2,128,16,32]{1,3,2,0:T(8,128)S(1)} fusion(f32[2,128,16,32]{1,3,2,0:T(8,128)S(1)} %copy-done.6, s32[]{:T(128)} %get-tuple-element.204, f32[16,32,32,32]{1,2,3,0:T(8,128)} %copy.39, f32[128,32,32]{0,1,2:T(8,128)S(1)} %get-tuple-element.222), kind=kOutput, calls=%fused_computation.14.clone.1 | convolution fusion | flops 805371904 | bytes 2883588 | tf_op jit(solution)/shard_map/while/body/eval_jaxpr/ijcd,sjd->sic/dot_general | solution.py:31
  205.7 0.8 copy-done.7
  206.5 0.0 all-reduce.7.cloned.1.call-update
  206.6 0.0 all-reduce.5.cloned.1.call-start
  206.6 52.6 %all-reduce.7.cloned.1.call-done = (f32[128,32,32]{0,2,1:T(8,128)}, f32[1024,128]{1,0:T(8,128)}) async-done(((f32[128,32,32]{0,2,1:T(8,128)}, f32[1024,128]{1,0:T(8,128)}), (f32[128,32,32]{0,2,1:T(8,128)}, f32[1024,128]{1,0:T(8,128)})) %all-reduce.7.cloned.1.call-update) | async-done | bytes 1048592 | tf_op jit(solution)/shard_map/psum | solution.py:49
  259.2 0.0 all-reduce.5.cloned.1.call-update
  259.2 1.2 reduce_sum.9
  260.4 10.0 %psum.46 = f32[128]{0:T(128)S(1)} all-reduce(f32[128]{0:T(128)S(1)} %reduce_sum.9), channel_id=1, replica_groups=mesh['row'=8,'col'=4] {'col'}, use_global_device_ids=true, to_apply=%region_7.8 | all-reduce | flops 128 | bytes 1024 | tf_op jit(solution)/shard_map/psum | solution.py:59
  270.4 11.8 %psum.47 = f32[128]{0:T(128)S(1)} all-reduce(f32[128]{0:T(128)S(1)} %psum.46), channel_id=1, replica_groups=mesh['row'=8,'col'=4] {'row'}, use_global_device_ids=true, to_apply=%region_8.9 | all-reduce | flops 128 | bytes 1024 | tf_op jit(solution)/shard_map/psum | solution.py:60
  282.3 0.5 broadcast_multiply_fusion.1
  282.8 1.6 constant_dynamic-slice_fusion.1
  284.4 34.1 %all-reduce.5.cloned.1.call-done = (f32[128,32,32]{0,2,1:T(8,128)}, f32[1024,128]{1,0:T(8,128)}) async-done(((f32[128,32,32]{0,2,1:T(8,128)}, f32[1024,128]{1,0:T(8,128)}), (f32[128,32,32]{0,2,1:T(8,128)}, f32[1024,128]{1,0:T(8,128)})) %all-reduce.5.cloned.1.call-update) | async-done | bytes 1048592 | tf_op jit(solution)/shard_map/psum | solution.py:50
  318.5 1.9 broadcast_multiply_fusion
  320.3 1.5 constant_dynamic-slice_fusion
  (25 shorter events, 0.0 us)
Async XLA Ops:
  7.2 252.0 %all-reduce.7.cloned.1.call-start = ((), (), s32[]{:S(2)}) async-start(), calls=%async_computation.1 | async-start | bytes 2097152 | tf_op jit(solution)/shard_map/psum | solution.py:49
  59.1 0.8 copy-start.2
  68.9 12.0 %copy-start.1 = (f32[1024,128]{1,0:T(8,128)S(1)}, f32[1024,128]{1,0:T(8,128)}, u32[]{:S(2)}) copy-start(f32[1024,128]{1,0:T(8,128)} %get-tuple-element.224) | copy-start | bytes 1572868 | tf_op jit(solution)/shard_map/while
  75.6 16.1 %copy-start.4 = (f32[128,32,32]{0,2,1:T(8,128)S(1)}, f32[128,32,32]{0,2,1:T(8,128)}, u32[]{:S(2)}) copy-start(f32[128,32,32]{0,2,1:T(8,128)} %get-tuple-element.206) | copy-start | bytes 1572868 | tf_op jit(solution)/shard_map/while
  80.9 28.7 %copy-start.8 = (f32[128]{0:T(128)S(1)}, f32[128]{0:T(128)}, u32[]{:S(2)}) copy-start(f32[128]{0:T(128)} %get-tuple-element.225) | copy-start | bytes 1540 | tf_op jit(solution)/shard_map/while
  88.6 3.2 copy-start
  108.8 0.8 copy-start.5
  112.1 10.6 %copy-start.6 = (f32[2,128,16,32]{1,3,2,0:T(8,128)S(1)}, f32[2,128,16,32]{1,3,2,0:T(8,128)}, u32[]{:S(2)}) copy-start(f32[2,128,16,32]{1,3,2,0:T(8,128)} %get-tuple-element.208) | copy-start | bytes 1572868 | tf_op jit(solution)/shard_map/while
  122.7 10.0 %copy-start.3 = (f32[2,128,16,32]{1,3,2,0:T(8,128)S(1)}, f32[2,128,16,32]{1,3,2,0:T(8,128)}, u32[]{:S(2)}) copy-start(f32[2,128,16,32]{1,3,2,0:T(8,128)} %copy-done.2) | copy-start | bytes 1572868 | tf_op jit(solution)/shard_map/while
  131.9 0.8 copy-start.7
  132.7 0.8 copy-start.2
  142.6 12.1 %copy-start.1 = (f32[1024,128]{1,0:T(8,128)S(1)}, f32[1024,128]{1,0:T(8,128)}, u32[]{:S(2)}) copy-start(f32[1024,128]{1,0:T(8,128)} %get-tuple-element.224) | copy-start | bytes 1572868 | tf_op jit(solution)/shard_map/while
  149.3 16.3 %copy-start.4 = (f32[128,32,32]{0,2,1:T(8,128)S(1)}, f32[128,32,32]{0,2,1:T(8,128)}, u32[]{:S(2)}) copy-start(f32[128,32,32]{0,2,1:T(8,128)} %get-tuple-element.206) | copy-start | bytes 1572868 | tf_op jit(solution)/shard_map/while
  154.7 28.7 %copy-start.8 = (f32[128]{0:T(128)S(1)}, f32[128]{0:T(128)}, u32[]{:S(2)}) copy-start(f32[128]{0:T(128)} %get-tuple-element.225) | copy-start | bytes 1540 | tf_op jit(solution)/shard_map/while
  162.4 3.2 copy-start
  182.6 0.8 copy-start.5
  185.9 10.6 %copy-start.6 = (f32[2,128,16,32]{1,3,2,0:T(8,128)S(1)}, f32[2,128,16,32]{1,3,2,0:T(8,128)}, u32[]{:S(2)}) copy-start(f32[2,128,16,32]{1,3,2,0:T(8,128)} %get-tuple-element.208) | copy-start | bytes 1572868 | tf_op jit(solution)/shard_map/while
  196.5 10.0 %copy-start.3 = (f32[2,128,16,32]{1,3,2,0:T(8,128)S(1)}, f32[2,128,16,32]{1,3,2,0:T(8,128)}, u32[]{:S(2)}) copy-start(f32[2,128,16,32]{1,3,2,0:T(8,128)} %copy-done.2) | copy-start | bytes 1572868 | tf_op jit(solution)/shard_map/while
  205.7 0.8 copy-start.7
  206.6 111.9 %all-reduce.5.cloned.1.call-start = ((), (), s32[]{:S(2)}) async-start(), calls=%async_computation | async-start | bytes 2097152 | tf_op jit(solution)/shard_map/psum | solution.py:50
Sparse Core Ops, SparseCore 0:
  206.7 52.4 all-reduce.6
  262.4 56.0 all-reduce.4
where the time goes:
time: 332 us; the launch traced here: 329 us
  matrix products  101 us (30%)
  waiting for transfers between devices  86.7 us (26%)
  blocking collectives  50 us (15%)
  local copies, waits for them, and re-layouts  49.2 us (15%)
  loops' own time  23.5 us (7%)
  between operations  14.5 us (4%)
  other arithmetic  3.58 us (1%)
    psum x1, waiting for transfers between devices, per_device(): left_total = lax.psum(left_part, 'col')  52.6 us
    psum x1, waiting for transfers between devices, per_device(): right_total = lax.psum(right_part, 'row')  34.1 us
    dot_general x2, matrix products, visit(): jnp.einsum('ijcd,sic->sjd', grad_outer, left_block, precision=high)  33.9 us
    another operation x1, loops' own time, per_device(): lax.scan(visit, start, (left_blocks, cot_blocks))  23.5 us
    dot_general x2, local copies, waits for them, and re-layouts, visit(): grad_flat = jnp.einsum('ije,ke->ijk', cot_block, weight, precision=high)  21.3 us
    dot_general x2, matrix products, visit(): jnp.einsum('ijcd,sjd->sic', grad_outer, right_all, precision=high) / samples  18.4 us
    dot_general x2, matrix products, visit(): jnp.einsum('sic,sjd->ijcd', left_block, right_all, precision=high) / samples  18.1 us
    all_gather x1, blocking collectives, per_device(): left_all = lax.all_gather(left_factors, 'col', axis=1, tiled=True)  16.6 us
  transfers between devices with their start and end apart: 2, of which 2 were waited for; matrix products, arithmetic and copies ran while one was open for 1% of the time, Pallas kernels for 0%

commit v1 on v0

--- a/solution.py
+++ b/solution.py
@@ -1,7 +1,15 @@
+import functools
 import jax
 import jax.numpy as jnp
 from jax import lax
 from jax.sharding import PartitionSpec as P
+
+
+def strips_all_lift(values, group_axis):
+    return lax.all_gather(values, axis_name=group_axis).sum(axis=0)
+
+
+pass_sheets_in = functools.partial(strips_all_lift, group_axis="row")
 
 
 def per_device(left_factors, right_factors, weight, bias, cotangent):
@@ -47,7 +55,7 @@
     left_part = left_pieces.transpose(1, 0, 2, 3).reshape(samples, tile_rows, width)
     bias_part = jnp.sum(cotangent, axis=(0, 1))
     left_total = lax.psum(left_part, "col")
-    right_total = lax.psum(right_part, "row")
+    right_total = pass_sheets_in(right_part)
     left_share = tile_rows // lax.axis_size("col")
     right_share = tile_cols // lax.axis_size("row")
     left_grad = lax.dynamic_slice_in_dim(

time: 332 us -> 374 us (1.13)
  waiting for transfers between devices: 86.7 us -> 122 us
  local copies, waits for them, and re-layouts: 49.2 us -> 53.6 us
    all_gather x0 -> x1, waiting for transfers between devices: none -> 36.7 us  [strips_all_lift(): return lax.all_gather(values, axis_name=group_axis).sum(axis=0)]
    unnamed x1 -> x2, local copies, waits for them, and re-layouts: 0.31 us -> 5.48 us
    while x36 -> x44, local copies, waits for them, and re-layouts: 11.2 us -> 11.3 us
  transfers between devices with their start and end apart: 2 -> 3, of which waited for: 2 -> 3; matrix products, arithmetic and copies ran while one was open for 1% -> 1% of each run, Pallas kernels for 0% -> 0%
where the time goes in v1:
time: 374 us; the launch traced here: 372 us
  waiting for transfers between devices  122 us (33%)
  matrix products  100 us (27%)
  local copies, waits for them, and re-layouts  53.6 us (14%)
  blocking collectives  49.5 us (13%)
  loops' own time  26.2 us (7%)
  between operations  14 us (4%)
  other arithmetic  6.77 us (2%)
    psum x1, waiting for transfers between devices, per_device(): left_total = lax.psum(left_part, 'col')  52.8 us
    all_gather x1, waiting for transfers between devices, strips_all_lift(): return lax.all_gather(values, axis_name=group_axis).sum(axis=0)  36.7 us
    dot_general x2, matrix products, visit(): jnp.einsum('ijcd,sic->sjd', grad_outer, left_block, precision=high)  33.9 us
    psum x1, waiting for transfers between devices, per_device(): weight_total, bias_total = lax.psum((weight_half, bias_half), 'row')  31.3 us
    another operation x1, loops' own time, per_device(): lax.scan(visit, start, (left_blocks, cot_blocks))  26.2 us
    dot_general x2, local copies, waits for them, and re-layouts, visit(): grad_flat = jnp.einsum('ije,ke->ijk', cot_block, weight, precision=high)  21.3 us
    dot_general x2, matrix products, visit(): jnp.einsum('ijcd,sjd->sic', grad_outer, right_all, precision=high) / samples  18.4 us
    dot_general x2, matrix products, visit(): jnp.einsum('sic,sjd->ijcd', left_block, right_all, precision=high) / samples  18.1 us
  transfers between devices with their start and end apart: 3, of which 3 were waited for; matrix products, arithmetic and copies ran while one was open for 1% of the time, Pallas kernels for 0%

profile of v1, /device:TPU:0, one launch (start us, length us, event | category | flops | bytes accessed | tf_op | source)
XLA Modules:
  0.0 371.9 jit_solution(4431208736060663664)
XLA Ops:
  7.2 0.0 all-reduce.6.cloned.1.call-start
  7.2 17.6 %all_gather.12 = f32[128,32,32]{0,2,1:T(8,128)S(1)} all-gather(f32[128,8,32]{0,2,1:T(8,128)} %param.7), channel_id=1, replica_groups=mesh['row'=8,'col'=4] {'col'}, dimensions={1}, use_global_device_ids=true | all-gather | bytes 655360 | tf_op jit(solution)/shard_map/all_gather | solution.py:20
  24.8 10.1 %all_gather.13 = f32[128,32,32]{0,2,1:T(8,128)S(1)} all-gather(f32[128,4,32]{0,2,1:T(8,128)} %param.8), channel_id=1, replica_groups=mesh['row'=8,'col'=4] {'row'}, dimensions={1}, use_global_device_ids=true | all-gather | bytes 589824 | tf_op jit(solution)/shard_map/all_gather | solution.py:21
  35.0 0.3 copy.17
  35.3 172.2 %while.17 = (s32[]{:T(128)}, f32[1024,128]{1,0:T(8,128)}, f32[128,32,32]{0,2,1:T(8,128)}, f32[2,16,32,128]{3,2,1,0:T(8,128)}, f32[2,128,16,32]{1,3,2,0:T(8,128)}...) while((s32[]{:T(128)}, f32[1024,128]{1,0:T(8,128)}, ...), condition=%wide.region_1.2_spmd.clone, body=%wide.region_0.1_spmd.clone.sunk | while | flops 4833148928 | bytes 54004692 | solution.py:51
  58.6 0.8 copy-done.2
  59.4 9.0 %multiply_bitcast_fusion.2 = f32[16,32,32,32]{3,2,1,0:T(8,128)} fusion(f32[128,32,32]{0,1,2:T(8,128)S(1)} %get-tuple-element.220, f32[2,128,16,32]{1,3,2,0:T(8,128)S(1)} %get-tuple-element.219, s32[]{:T(128)S(6)} %copy.49), kind=kOutput, calls=%fused_computation.2.clone.1 | convolution fusion | flops 805830656 | bytes 2883588 | tf_op jit(solution)/shard_map/while/body/eval_jaxpr/sic,sjd->ijcd/dot_general | solution.py:32
  68.4 6.7 %reshape.44 = f32[16,32,1024]{2,1,0:T(8,128)S(1)} reshape(f32[16,32,32,32]{3,2,1,0:T(8,128)} %multiply_bitcast_fusion.2) | data formatting | bytes 4194304 | tf_op jit(solution)/shard_map/while/body/eval_jaxpr/reshape | solution.py:33
  75.1 5.2 %fusion.67 = f32[1024,128]{1,0:T(8,128)} fusion(f32[16,32,1024]{2,1,0:T(8,128)S(1)} %reshape.44, f32[1024,128]{1,0:T(8,128)} %get-tuple-element.203, pred[]{:T(512)S(6)} %compare.3, f32[2,16,32,128]{3,2,1,0:T(8,128)} %get-tuple-element.221, s32[]{:T(128)S(6)} %copy.49), kind=kOutput, calls=%fused_computation.5.clone.1 | convolution fusion | flops 805568512 | bytes 3407877 | tf_op jit(solution)/shard_map/while/body/eval_jaxpr/ijk,ije->ke/dot_general | solution.py:36
  80.4 7.7 %fusion.68 = f32[16,32,32,32]{3,1,2,0:T(8,128)S(1)} fusion(f32[32,32,128,1]{2,1,0,3:T(8,128)S(1)} %bitcast.116, f32[2,16,32,128]{3,2,1,0:T(8,128)} %get-tuple-element.221, s32[]{:T(128)S(6)} %copy.49), kind=kOutput, calls=%fused_computation.19.clone.1 | convolution fusion | flops 805306368 | bytes 2883588 | tf_op jit(solution)/shard_map/while/body/eval_jaxpr/ije,ke->ijk/dot_general | solution.py:35
  88.1 3.2 copy-done
  91.3 17.0 %fusion.69 = f32[128,32,32]{0,2,1:T(8,128)S(1)} fusion(f32[16,32,32,32]{3,1,2,0:T(8,128)S(1)} %fusion.68, f32[128,32,32]{0,2,1:T(8,128)S(1)} %copy-done.4, pred[]{:T(512)S(6)} %compare.3, f32[2,128,16,32]{1,3,2,0:T(8,128)} %copy-done.2, s32[]{:T(128)S(6)} %copy.49), kind=kOutput, calls=%fused_computation.7.clone.1 | convolution fusion | flops 805699584 | bytes 3407877 | tf_op jit(solution)/shard_map/while/body/eval_jaxpr/ijcd,sic->sjd/dot_general | solution.py:43
  108.3 1.8 fusion.70
  110.2 0.0 copy-start.10
  110.2 0.8 copy-done.10
  111.0 10.6 %copy.41 = f32[16,32,32,32]{1,2,3,0:T(8,128)} copy(f32[16,32,32,32]{3,1,2,0:T(8,128)} %copy-done) | data formatting | bytes 4194304 | tf_op jit(solution)/shard_map/while/body/eval_jaxpr/ije,ke->ijk/dot_general | solution.py:35
  121.6 9.2 %fusion.71 = f32[2,128,16,32]{1,3,2,0:T(8,128)S(1)} fusion(f32[2,128,16,32]{1,3,2,0:T(8,128)S(1)} %copy-done.6, s32[]{:T(128)S(6)} %copy.49, f32[16,32,32,32]{1,2,3,0:T(8,128)} %copy.41, f32[128,32,32]{0,1,2:T(8,128)S(1)} %get-tuple-element.220), kind=kOutput, calls=%fused_computation.14.clone.1 | convolution fusion | flops 805371904 | bytes 2883588 | tf_op jit(solution)/shard_map/while/body/eval_jaxpr/ijcd,sjd->sic/dot_general | solution.py:39
  130.8 0.8 copy-done.7
  131.6 0.8 copy-done.2
  132.4 9.0 %multiply_bitcast_fusion.2 = f32[16,32,32,32]{3,2,1,0:T(8,128)} fusion(f32[128,32,32]{0,1,2:T(8,128)S(1)} %get-tuple-element.220, f32[2,128,16,32]{1,3,2,0:T(8,128)S(1)} %get-tuple-element.219, s32[]{:T(128)S(6)} %copy.49), kind=kOutput, calls=%fused_computation.2.clone.1 | convolution fusion | flops 805830656 | bytes 2883588 | tf_op jit(solution)/shard_map/while/body/eval_jaxpr/sic,sjd->ijcd/dot_general | solution.py:32
  141.5 6.7 %reshape.44 = f32[16,32,1024]{2,1,0:T(8,128)S(1)} reshape(f32[16,32,32,32]{3,2,1,0:T(8,128)} %multiply_bitcast_fusion.2) | data formatting | bytes 4194304 | tf_op jit(solution)/shard_map/while/body/eval_jaxpr/reshape | solution.py:33
  148.2 5.4 %fusion.67 = f32[1024,128]{1,0:T(8,128)} fusion(f32[16,32,1024]{2,1,0:T(8,128)S(1)} %reshape.44, f32[1024,128]{1,0:T(8,128)} %get-tuple-element.203, pred[]{:T(512)S(6)} %compare.3, f32[2,16,32,128]{3,2,1,0:T(8,128)} %get-tuple-element.221, s32[]{:T(128)S(6)} %copy.49), kind=kOutput, calls=%fused_computation.5.clone.1 | convolution fusion | flops 805568512 | bytes 3407877 | tf_op jit(solution)/shard_map/while/body/eval_jaxpr/ijk,ije->ke/dot_general | solution.py:36
  153.6 7.7 %fusion.68 = f32[16,32,32,32]{3,1,2,0:T(8,128)S(1)} fusion(f32[32,32,128,1]{2,1,0,3:T(8,128)S(1)} %bitcast.116, f32[2,16,32,128]{3,2,1,0:T(8,128)} %get-tuple-element.221, s32[]{:T(128)S(6)} %copy.49), kind=kOutput, calls=%fused_computation.19.clone.1 | convolution fusion | flops 805306368 | bytes 2883588 | tf_op jit(solution)/shard_map/while/body/eval_jaxpr/ije,ke->ijk/dot_general | solution.py:35
  161.3 3.2 copy-done
  164.5 17.0 %fusion.69 = f32[128,32,32]{0,2,1:T(8,128)S(1)} fusion(f32[16,32,32,32]{3,1,2,0:T(8,128)S(1)} %fusion.68, f32[128,32,32]{0,2,1:T(8,128)S(1)} %copy-done.4, pred[]{:T(512)S(6)} %compare.3, f32[2,128,16,32]{1,3,2,0:T(8,128)} %copy-done.2, s32[]{:T(128)S(6)} %copy.49), kind=kOutput, calls=%fused_computation.7.clone.1 | convolution fusion | flops 805699584 | bytes 3407877 | tf_op jit(solution)/shard_map/while/body/eval_jaxpr/ijcd,sic->sjd/dot_general | solution.py:43
  181.5 1.8 fusion.70
  183.4 0.0 copy-start.10
  183.4 0.8 copy-done.10
  184.2 10.6 %copy.41 = f32[16,32,32,32]{1,2,3,0:T(8,128)} copy(f32[16,32,32,32]{3,1,2,0:T(8,128)} %copy-done) | data formatting | bytes 4194304 | tf_op jit(solution)/shard_map/while/body/eval_jaxpr/ije,ke->ijk/dot_general | solution.py:35
  194.8 9.2 %fusion.71 = f32[2,128,16,32]{1,3,2,0:T(8,128)S(1)} fusion(f32[2,128,16,32]{1,3,2,0:T(8,128)S(1)} %copy-done.6, s32[]{:T(128)S(6)} %copy.49, f32[16,32,32,32]{1,2,3,0:T(8,128)} %copy.41, f32[128,32,32]{0,1,2:T(8,128)S(1)} %get-tuple-element.220), kind=kOutput, calls=%fused_computation.14.clone.1 | convolution fusion | flops 805371904 | bytes 2883588 | tf_op jit(solution)/shard_map/while/body/eval_jaxpr/ijcd,sjd->sic/dot_general | solution.py:39
  204.0 0.8 copy-done.7
  207.5 0.0 all-reduce.6.cloned.1.call-update
  207.5 0.0 all-reduce.4.cloned.1.call-start
  207.5 52.8 %all-reduce.6.cloned.1.call-done = (f32[128,32,32]{0,2,1:T(8,128)}, f32[1024,128]{1,0:T(8,128)}) async-done(((f32[128,32,32]{0,2,1:T(8,128)}, f32[1024,128]{1,0:T(8,128)}), (f32[128,32,32]{0,2,1:T(8,128)}, f32[1024,128]{1,0:T(8,128)})) %all-reduce.6.cloned.1.call-update) | async-done | bytes 1048592 | tf_op jit(solution)/shard_map/psum | solution.py:57
  260.4 0.0 all-reduce.4.cloned.1.call-update
  260.4 0.0 all-gather.3.cloned.1.call-start
  260.4 0.7 all-gather.3.cloned.1.call-update
  261.1 1.2 reduce_sum.19
  262.3 10.0 %psum.38 = f32[128]{0:T(128)S(1)} all-reduce(f32[128]{0:T(128)S(1)} %reduce_sum.19), channel_id=1, replica_groups=mesh['row'=8,'col'=4] {'col'}, use_global_device_ids=true, to_apply=%region_7.8 | all-reduce | flops 128 | bytes 1024 | tf_op jit(solution)/shard_map/psum | solution.py:67
  272.3 11.8 %psum.39 = f32[128]{0:T(128)S(1)} all-reduce(f32[128]{0:T(128)S(1)} %psum.38), channel_id=1, replica_groups=mesh['row'=8,'col'=4] {'row'}, use_global_device_ids=true, to_apply=%region_8.9 | all-reduce | flops 128 | bytes 1024 | tf_op jit(solution)/shard_map/psum | solution.py:68
  284.2 0.5 broadcast_multiply_fusion.1
  284.7 1.6 constant_dynamic-slice_fusion.1
  286.2 31.3 %all-reduce.4.cloned.1.call-done = f32[1024,128]{1,0:T(8,128)} async-done(((f32[1024,128]{1,0:T(8,128)}), f32[1024,128]{1,0:T(8,128)}) %all-reduce.4.cloned.1.call-update) | async-done | bytes 524304 | tf_op jit(solution)/shard_map/psum | solution.py:68
  317.6 1.9 broadcast_multiply_fusion
  319.4 36.7 %all-gather.3.cloned.1.call-done = f32[1024,32,32]{0,2,1:T(8,128)} async-done(((f32[128,32,32]{0,2,1:T(8,128)}), f32[1024,32,32]{0,2,1:T(8,128)}) %all-gather.3.cloned.1.call-update) | async-done | bytes 4194320 | tf_op jit(solution)/shard_map/all_gather | solution.py:9
  356.1 5.2 %copy.22 = f32[128,8,8,128]{3,2,1,0:T(8,128)} copy(f32[128,8,8,128]{3,1,2,0:T(8,128)} %bitcast.121) | data formatting | bytes 8388608
  361.3 3.2 reduce_sum.18
  364.5 0.6 constant_dynamic-slice_fusion
  (38 shorter events, 0.1 us)
Async XLA Ops:
  7.2 253.2 %all-reduce.6.cloned.1.call-start = ((), (), s32[]{:S(2)}) async-start(), calls=%async_computation.2 | async-start | bytes 2097152 | tf_op jit(solution)/shard_map/psum | solution.py:57
  58.6 0.8 copy-start.2
  68.4 12.0 %copy-start.1 = (f32[1024,128]{1,0:T(8,128)S(1)}, f32[1024,128]{1,0:T(8,128)}, u32[]{:S(2)}) copy-start(f32[1024,128]{1,0:T(8,128)} %get-tuple-element.222) | copy-start | bytes 1572868 | tf_op jit(solution)/shard_map/while
  75.1 16.2 %copy-start.4 = (f32[128,32,32]{0,2,1:T(8,128)S(1)}, f32[128,32,32]{0,2,1:T(8,128)}, u32[]{:S(2)}) copy-start(f32[128,32,32]{0,2,1:T(8,128)} %get-tuple-element.204) | copy-start | bytes 1572868 | tf_op jit(solution)/shard_map/while
  80.4 27.9 %copy-start.8 = (f32[128]{0:T(128)S(1)}, f32[128]{0:T(128)}, u32[]{:S(2)}) copy-start(f32[128]{0:T(128)} %get-tuple-element.223) | copy-start | bytes 1540 | tf_op jit(solution)/shard_map/while
  80.4 27.9 %copy-start.9 = (f32[2,16,32,128]{3,2,1,0:T(8,128)S(1)}, f32[2,16,32,128]{3,2,1,0:T(8,128)}, u32[]{:S(2)}) copy-start(f32[2,16,32,128]{3,2,1,0:T(8,128)} %get-tuple-element.205) | copy-start | bytes 1572868 | tf_op jit(solution)/shard_map/while
  88.1 3.2 copy-start
  108.3 1.8 copy-start.5
  110.2 0.8 copy-start.10
  110.9 10.6 %copy-start.6 = (f32[2,128,16,32]{1,3,2,0:T(8,128)S(1)}, f32[2,128,16,32]{1,3,2,0:T(8,128)}, u32[]{:S(2)}) copy-start(f32[2,128,16,32]{1,3,2,0:T(8,128)} %get-tuple-element.206) | copy-start | bytes 1572868 | tf_op jit(solution)/shard_map/while
  121.6 10.0 %copy-start.3 = (f32[2,128,16,32]{1,3,2,0:T(8,128)S(1)}, f32[2,128,16,32]{1,3,2,0:T(8,128)}, u32[]{:S(2)}) copy-start(f32[2,128,16,32]{1,3,2,0:T(8,128)} %copy-done.2) | copy-start | bytes 1572868 | tf_op jit(solution)/shard_map/while
  130.8 0.8 copy-start.7
  131.6 0.8 copy-start.2
  141.5 12.1 %copy-start.1 = (f32[1024,128]{1,0:T(8,128)S(1)}, f32[1024,128]{1,0:T(8,128)}, u32[]{:S(2)}) copy-start(f32[1024,128]{1,0:T(8,128)} %get-tuple-element.222) | copy-start | bytes 1572868 | tf_op jit(solution)/shard_map/while
  148.2 16.4 %copy-start.4 = (f32[128,32,32]{0,2,1:T(8,128)S(1)}, f32[128,32,32]{0,2,1:T(8,128)}, u32[]{:S(2)}) copy-start(f32[128,32,32]{0,2,1:T(8,128)} %get-tuple-element.204) | copy-start | bytes 1572868 | tf_op jit(solution)/shard_map/while
  153.6 27.9 %copy-start.8 = (f32[128]{0:T(128)S(1)}, f32[128]{0:T(128)}, u32[]{:S(2)}) copy-start(f32[128]{0:T(128)} %get-tuple-element.223) | copy-start | bytes 1540 | tf_op jit(solution)/shard_map/while
  153.6 27.9 %copy-start.9 = (f32[2,16,32,128]{3,2,1,0:T(8,128)S(1)}, f32[2,16,32,128]{3,2,1,0:T(8,128)}, u32[]{:S(2)}) copy-start(f32[2,16,32,128]{3,2,1,0:T(8,128)} %get-tuple-element.205) | copy-start | bytes 1572868 | tf_op jit(solution)/shard_map/while
  161.3 3.2 copy-start
  181.5 1.8 copy-start.5
  183.4 0.8 copy-start.10
  184.2 10.6 %copy-start.6 = (f32[2,128,16,32]{1,3,2,0:T(8,128)S(1)}, f32[2,128,16,32]{1,3,2,0:T(8,128)}, u32[]{:S(2)}) copy-start(f32[2,128,16,32]{1,3,2,0:T(8,128)} %get-tuple-element.206) | copy-start | bytes 1572868 | tf_op jit(solution)/shard_map/while
  194.8 10.0 %copy-start.3 = (f32[2,128,16,32]{1,3,2,0:T(8,128)S(1)}, f32[2,128,16,32]{1,3,2,0:T(8,128)}, u32[]{:S(2)}) copy-start(f32[2,128,16,32]{1,3,2,0:T(8,128)} %copy-done.2) | copy-start | bytes 1572868 | tf_op jit(solution)/shard_map/while
  204.0 0.8 copy-start.7
  207.5 110.1 %all-reduce.4.cloned.1.call-start = ((), (), s32[]{:S(2)}) async-start(), calls=%async_computation | async-start | bytes 1048576 | tf_op jit(solution)/shard_map/psum | solution.py:68
  260.4 95.7 %all-gather.3.cloned.1.call-start = ((), (), s32[]{:S(2)}) async-start(), calls=%async_computation.1 | async-start | bytes 4718592 | tf_op jit(solution)/shard_map/all_gather | solution.py:9
Sparse Core Ops, SparseCore 0:
  207.6 52.7 all-reduce.5
  263.5 54.0 all-reduce.3
  319.4 36.6 all-gather.2
